TPU v7x, 256 devices: a whole 4x4x8 slice. The times are simulated.
256 devices in a mesh: member: 32 (over x, y, core), grid: 8 (over z).
Axes of the slice: x: 4, y: 4, z: 8, core: 2. Of those that a mesh axis runs over, the one named last changes fastest.
Arguments:
- prior_ensemble: bfloat16 [512, 48, 32768], P('member', None, 'grid'), may hold values from -6 to 6
- measured_location: int32 [8, 32, 128], P('grid', 'member'), may hold values from 0 to 6143
- measured_tally: int32 [8, 32], P('grid', 'member'), may hold values from 32 to 128, as said below
- measured_reading: float32 [8, 32, 128], P('grid', 'member'), may hold values from -6 to 6
- measured_noise_sigma: float32 [8, 32, 128], P('grid', 'member'), may hold values from 0.5 to 20, as said below
Outputs:
- analysis: bfloat16 [512, 48, 32768], P('member', None, 'grid')
Inputs may be any that keep to these rules, and one draw needn't show every extreme that they name: `measured_location`: cell of the observation within its block of 48 rows and 128 columns. `measured_tally`: some block in every draw uses all 128 slots. `measured_noise_sigma`: positive error deviations.
All inputs are finite; a program needn't handle non-finite values.
Results may differ from a plain program's by a relative error of at most 0.0058.
Values may be sent and summed in bfloat16 or wider, within the bound.
A program may use at most 128 MiB of HBM per device.

v0:
```python
import jax
import jax.numpy as jnp
from jax import lax
from jax.sharding import PartitionSpec as P

HIGHEST_PRECISION = lax.Precision.HIGHEST


def whiten(hx_values, values, errors, obs_total):
    hx_float = hx_values.astype(jnp.float32)
    hx_mean = jnp.mean(hx_float, axis=0)
    usable = (jnp.arange(hx_values.shape[1], dtype=jnp.int32) < obs_total).astype(jnp.float32)
    scale_obs = usable / errors
    whitened = (hx_float - hx_mean) * scale_obs
    innovation = (values - hx_mean) * scale_obs
    return (whitened, innovation)


def transform_matrix(gram_total, drive_vector):
    members = gram_total.shape[0]
    identity = jnp.eye(members, dtype=jnp.float32)
    system = (members - 1.0) * identity + gram_total
    factor_low = jnp.linalg.cholesky(system)
    inverse = jax.scipy.linalg.solve_triangular(factor_low, identity, lower=True)
    inner = jnp.dot(inverse, drive_vector, precision=HIGHEST_PRECISION)
    mean_weight = jnp.dot(inverse.T, inner, precision=HIGHEST_PRECISION)
    spread = jnp.sqrt(members - 1.0) * inverse.T
    return (mean_weight[:, None] + spread).astype(jnp.bfloat16)


def local_sums(whitened, innovation):
    gram_local = lax.dot_general(
        whitened, whitened, (((1,), (1,)), ((), ())), precision=HIGHEST_PRECISION
    )
    drive_local = jnp.dot(whitened, innovation, precision=HIGHEST_PRECISION)
    return (gram_local, drive_local)


def reduce_gram(whitened, innovation):
    gram_local, drive_local = local_sums(whitened, innovation)
    gram_total, drive_vector = lax.psum((gram_local, drive_local), ("member", "grid"))
    return transform_matrix(gram_total, drive_vector)


def apply_block(state_block, transform):
    members, row_count, columns = state_block.shape
    flattened = state_block.reshape(members, row_count * columns)
    state_mean = jnp.mean(flattened.astype(jnp.float32), axis=0)
    anomalies = (flattened.astype(jnp.float32) - state_mean).astype(jnp.bfloat16)
    increment = lax.dot_general(
        transform, anomalies, (((0,), (0,)), ((), ())), preferred_element_type=jnp.float32
    )
    return (state_mean + increment).astype(jnp.bfloat16).reshape(members, row_count, columns)


def local(
    prior_ensemble, measured_location, measured_tally, measured_reading, measured_noise_sigma
):
    values = measured_reading[0, 0]
    errors = measured_noise_sigma[0, 0]
    obs_total = measured_tally[0, 0]
    shard_profiles = lax.all_to_all(
        prior_ensemble, "member", split_axis=2, concat_axis=0, tiled=True
    )
    members, row_count, columns = shard_profiles.shape
    hx_values = jnp.take(
        shard_profiles.reshape(members, row_count * columns), measured_location[0, 0], axis=1
    )
    whitened, innovation = whiten(hx_values, values, errors, obs_total)
    transform = reduce_gram(whitened, innovation)
    updated = apply_block(shard_profiles, transform)
    return lax.all_to_all(updated, "member", split_axis=0, concat_axis=2, tiled=True)


def solution(mesh):
    in_specs = (
        P("member", None, "grid"),
        P("grid", "member", None),
        P("grid", "member"),
        P("grid", "member", None),
        P("grid", "member", None),
    )
    out_specs = P("member", None, "grid")
    return jax.shard_map(local, mesh=mesh, in_specs=in_specs, out_specs=out_specs, check_vma=False)
```

profile of v0, /device:TPU:1, one launch (start us, length us, event | category | flops | bytes accessed | tf_op | source)
XLA Modules:
  0.0 763.2 jit_solution(7519993507879228197)
XLA Ops:
  6.5 19.4 %copy.19 = bf16[16,48,4096]{1,0,2:T(8,128)(2,1)} copy(bf16[16,48,4096]{2,1,0:T(8,128)(2,1)} %param.5) | data formatting | bytes 12582912 | tf_op args[0]
  25.9 31.8 %reshape.139 = bf16[32,2,49152]{2,1,0:T(2,128)(2,1)} reshape(bf16[4096,16,48]{2,1,0:T(8,128)(2,1)} %bitcast.111) | data formatting | bytes 12582912
  57.7 8.8 %all-to-all-start = ((bf16[32,2,49152]{2,1,0:T(2,128)(2,1)}), bf16[32,2,49152]{2,1,0:T(2,128)(2,1)}, u32[]{:S(2)}, u32[]{:S(2)}) async-start(bf16[32,2,49152]{2,1,0:T(2,128)(2,1)} %reshape.139), calls=%async_computation | async-start | bytes 12582912 | tf_op jit(solution)/shard_map/all_to_all | solution.py:62
  68.9 74.8 %all-to-all-done = bf16[32,2,49152]{2,1,0:T(2,128)(2,1)} async-done(((bf16[32,2,49152]{2,1,0:T(2,128)(2,1)}), bf16[32,2,49152]{2,1,0:T(2,128)(2,1)}, u32[]{:S(2)}, u32[]{:S(2)}) %all-to-all-start) | async-done | bytes 6291488 | tf_op jit(solution)/shard_map/all_to_all | solution.py:62
  143.7 27.6 %reshape.140 = bf16[4096,16,48]{2,1,0:T(8,128)(2,1)} reshape(bf16[32,2,49152]{2,1,0:T(2,128)(2,1)} %all-to-all-done) | data formatting | bytes 12582912
  171.3 18.8 %copy.20 = bf16[16,48,32,128]{3,1,0,2:T(8,128)(2,1)} copy(bf16[16,48,32,128]{1,0,3,2:T(8,128)(2,1)} %bitcast.110) | data formatting | bytes 12582912 | tf_op jit(solution)/shard_map/all_to_all | solution.py:62
  190.1 7.1 copy.44
  197.1 8.7 %copy.21 = bf16[512,6144]{0,1:T(8,128)(2,1)} copy(bf16[512,6144]{1,0:T(8,128)(2,1)} %bitcast.119) | data formatting | bytes 12582912 | tf_op jit(solution)/shard_map/reshape | solution.py:47
  205.8 4.5 gather_fusion
  210.5 2.2 fusion.20
  213.1 89.1 %psum.15 = f32[512]{0:T(512)S(1)} all-reduce(f32[512]{0:T(512)S(1)} %bitcast.121), channel_id=1, replica_groups=mesh['member'=32,'grid'=8] {'member','grid'}, use_global_device_ids=true, to_apply=%region_11.12 | all-reduce | flops 512 | bytes 4096 | tf_op jit(solution)/shard_map/psum | solution.py:41
  302.2 4.1 convert_reduce_fusion
  306.9 173.6 %all-reduce.3.cloned.1.call-done = f32[512,512]{0,1:T(8,128)} async-done(((f32[512,512]{0,1:T(8,128)}), f32[512,512]{0,1:T(8,128)}) %all-reduce.3.cloned.1.call-update) | async-done | bytes 1048592 | tf_op jit(solution)/shard_map/psum | solution.py:41
  483.7 11.7 %cholesky.107 = f32[128,128]{1,0:T(8,128)S(1)} custom-call(f32[128,128]{1,0:T(8,128)S(1)} %cholesky.269), custom_call_target="Cholesky" | custom-call | tf_op jit(solution)/shard_map/jit(cholesky)/cholesky | solution.py:23
  495.4 9.8 %custom-call.31 = f32[1,128,128]{1,2,0:T(8,128)S(1)} custom-call(f32[1,128,128]{2,1,0:T(8,128)S(1)} %get-tuple-element.36), custom_call_target="InvertDiagBlocksLowerTriangular" | custom-call | tf_op jit(solution)/shard_map/jit(cholesky)/cholesky | solution.py:23
  505.9 11.9 %cholesky.221 = f32[128,128]{1,0:T(8,128)S(1)} custom-call(f32[128,128]{1,0:T(8,128)S(1)} %cholesky.273), custom_call_target="Cholesky" | custom-call | tf_op jit(solution)/shard_map/jit(cholesky)/cholesky | solution.py:23
  518.2 9.8 %custom-call.32 = f32[1,128,128]{1,2,0:T(8,128)S(1)} custom-call(f32[1,128,128]{2,1,0:T(8,128)S(1)} %get-tuple-element.34), custom_call_target="InvertDiagBlocksLowerTriangular" | custom-call | tf_op jit(solution)/shard_map/jit(cholesky)/cholesky | solution.py:23
  530.8 13.2 %cholesky.242 = f32[128,128]{1,0:T(8,128)} custom-call(f32[128,128]{1,0:T(8,128)} %cholesky.278), custom_call_target="Cholesky" | custom-call | tf_op jit(solution)/shard_map/jit(cholesky)/cholesky | solution.py:23
  547.8 11.3 %custom-call.33 = f32[1,128,128]{1,2,0:T(8,128)} custom-call(f32[1,128,128]{2,1,0:T(8,128)} %get-tuple-element.32), custom_call_target="InvertDiagBlocksLowerTriangular" | custom-call | tf_op jit(solution)/shard_map/jit(cholesky)/cholesky | solution.py:23
  561.5 11.9 %cholesky.259 = f32[128,128]{1,0:T(8,128)S(1)} custom-call(f32[128,128]{1,0:T(8,128)S(1)} %convolution_subtract_fusion.5), custom_call_target="Cholesky" | custom-call | tf_op jit(solution)/shard_map/jit(cholesky)/cholesky | solution.py:23
  581.8 14.5 %while.1 = (s32[]{:T(128)}, f32[512,512]{0,1:T(8,128)}, s32[4,2]{0,1:T(2,128)S(1)}, f32[4,128,128]{2,1,0:T(8,128)}, s32[]{:T(128)}) while((s32[]{:T(128)}, f32[512,512]{0,1:T(8,128)}, s32[4,2]{0,1:T(2,128)S(1)}, f32[4,128,128]{2,1,0:T(8,128)}, s32[]{:T(128)}) %tuple.25), condition=%wide.while_cond, body=%wide.while_body.sunk | while | flops 2 | bytes 393829 | solution.py:24
  582.5 2.2 dynamic-slice.7
  586.1 2.2 dynamic-slice.7
  589.8 2.2 dynamic-slice.7
  596.3 40.1 %custom-call.34 = f32[4,128,128]{1,2,0:T(8,128)S(1)} custom-call(f32[4,128,128]{2,1,0:T(8,128)} %get-tuple-element.12), custom_call_target="InvertDiagBlocksLowerTriangular" | custom-call | tf_op jit(solution)/shard_map/jit(_solve_triangular)/triangular_solve | solution.py:24
  638.8 2.2 convolution_subtract_fusion
  641.5 2.5 convolution_subtract_fusion.2
  646.1 6.8 fusion.1
  652.9 4.7 copy.38
  657.6 81.4 %all_to_all.33 = bf16[512,48,128]{2,1,0:T(8,128)(2,1)S(1)} all-to-all(bf16[512,48,128]{2,1,0:T(8,128)(2,1)S(1)} %bitcast.116), channel_id=1, replica_groups=mesh['member'=32,'grid'=8] {'member'}, dimensions={0} | all-to-all | bytes 12582912 | tf_op jit(solution)/shard_map/all_to_all | solution.py:72
  739.0 6.7 copy.45
  745.7 10.3 %all_to_all.30 = bf16[16,48,4096]{2,1,0:T(8,128)(2,1)} reshape(bf16[16,48,32,128]{3,2,1,0:T(8,128)(2,1)} %bitcast.118) | data formatting | bytes 12582912 | tf_op jit(solution)/shard_map/all_to_all | solution.py:72
  (84 shorter events, 34.6 us)
Async XLA Ops:
  57.6 10.1 %copy-start.3 = (s32[1,1,128]{2,1,0:T(1,128)S(1)}, s32[1,1,128]{2,1,0:T(1,128)}, u32[]{:S(2)}) copy-start(s32[1,1,128]{2,1,0:T(1,128)} %param.6) | copy-start | bytes 1540
  57.7 86.1 %all-to-all-start = ((bf16[32,2,49152]{2,1,0:T(2,128)(2,1)}), bf16[32,2,49152]{2,1,0:T(2,128)(2,1)}, u32[]{:S(2)}, u32[]{:S(2)}) async-start(bf16[32,2,49152]{2,1,0:T(2,128)(2,1)} %reshape.139), calls=%async_computation | async-start | bytes 12582912 | tf_op jit(solution)/shard_map/all_to_all | solution.py:62
  66.4 414.1 %all-reduce.3.cloned.1.call-start = ((), (), s32[]{:S(2)}) async-start(), calls=%async_computation.2 | async-start | bytes 2097152 | tf_op jit(solution)/shard_map/psum | solution.py:41
  197.1 13.3 %copy-start.2 = (f32[1,1,128]{2,1,0:T(1,128)S(1)}, f32[1,1,128]{2,1,0:T(1,128)}, u32[]{:S(2)}) copy-start(f32[1,1,128]{2,1,0:T(1,128)} %param.9) | copy-start | bytes 1540
  197.1 15.6 %copy-start.4 = (f32[1,1,128]{2,1,0:T(1,128)S(1)}, f32[1,1,128]{2,1,0:T(1,128)}, u32[]{:S(2)}) copy-start(f32[1,1,128]{2,1,0:T(1,128)} %param.8) | copy-start | bytes 1540
  483.6 44.5 %copy-start = (f32[512,512]{1,0:T(8,128)}, f32[512,512]{1,0:T(8,128)S(1)}, u32[]{:S(2)}) copy-start(f32[512,512]{1,0:T(8,128)S(1)} %fusion.6) | copy-start | bytes 3145732
  528.5 117.6 %slice-start = ((s8[6291456]{0:T(1024)(128)(4,1)}), s8[2097152]{0:T(1024)(128)(4,1)S(1)}, s32[]{:S(2)}) async-start(s8[6291456]{0:T(1024)(128)(4,1)} %bitcast.113), calls=%async_computation.3 | async-start | bytes 4194304
  580.0 66.1 %copy-start.1 = (f32[6144]{0:T(1024)S(1)}, f32[6144]{0:T(1024)}, u32[]{:S(2)}) copy-start(f32[6144]{0:T(1024)} %multiply_bitcast_fusion) | copy-start | bytes 73732
  638.4 7.7 %slice-start.1 = ((s8[6291456]{0:T(1024)(128)(4,1)}), s8[4194304]{0:T(1024)(128)(4,1)S(1)}, s32[]{:S(2)}) async-start(s8[6291456]{0:T(1024)(128)(4,1)} %bitcast.113), calls=%async_computation.4 | async-start | bytes 8388608
Sparse Core Ops, SparseCore 0:
  212.8 267.6 all-reduce.2
where the time goes:
time: 773 us; the launch traced here: 763 us
  waiting for transfers between devices  248 us (32%)
  blocking collectives  170 us (22%)
  local copies, waits for them, and re-layouts  158 us (20%)
  other arithmetic  136 us (18%)
  matrix products  24 us (3%)
  between operations  17.3 us (2%)
  starting transfers between devices  8.8 us (1%)
    psum x1, waiting for transfers between devices, reduce_gram(): lax.psum((gram_local, drive_local), ('member', 'grid'))  174 us
    unnamed x19, local copies, waits for them, and re-layouts  90.5 us
    psum x1, blocking collectives, reduce_gram(): lax.psum((gram_local, drive_local), ('member', 'grid'))  89.1 us
    another operation x15, other arithmetic, transform_matrix(): factor_low = jnp.linalg.cholesky(system)  85.1 us
    all_to_all x1, blocking collectives, local(): lax.all_to_all(updated, 'member', split_axis=0, concat_axis=2, tiled=True)  81.4 us
    all_to_all x1, waiting for transfers between devices, local(): lax.all_to_all(prior_ensemble, 'member', split_axis=2, concat_axis=0, til...  74.8 us
    another operation x3, other arithmetic, transform_matrix(): jax.scipy.linalg.solve_triangular(factor_low, identity, lower=True)  41.8 us
    all_to_all x1, local copies, waits for them, and re-layouts, local(): lax.all_to_all(prior_ensemble, 'member', split_axis=2, concat_axis=0, til...  18.8 us
  transfers between devices with their start and end apart: 2, of which 2 were waited for; matrix products, arithmetic and copies ran while one was open for 1% of the time, Pallas kernels for 0%

commit v1 on v0

v1 whole, which is shorter than its diff:
```python
import functools

import jax
import jax.numpy as jnp
from jax import lax
from jax.experimental import pallas as pl
from jax.experimental.pallas import tpu as pltpu
from jax.sharding import PartitionSpec as P

HIGHEST = lax.Precision.HIGHEST
MESH = pl.DeviceIdType.MESH
ANY = pl.ANY

N = 512
G = 32
B = N // G
Z = 8
R = 48
C = 128
OBS = 128
EXT = N + 128
SLAB = 8
SLABS = R // SLAB

ORDER = (8, 24, 16, 2, 6, 4, 1, 9, 25, 17, 3, 7, 5, 10, 26, 18, 11, 27, 19, 12, 28, 20, 13, 29, 21, 14, 30, 22, 15, 31, 23)


def peer_of(me, r):
    dx, dy, dc = r // 8, (r // 2) % 4, r % 2
    x, y, c = me // 8, (me // 2) % 4, me % 2
    s = 1 - 2 * c
    return ((x + s * dx + 4) % 4) * 8 + ((y + s * dy + 4) % 4) * 2 + (c + dc) % 2


def at_member(p):
    return {"member": p}


def at_grid(q):
    return {"grid": q}


def gather_kernel(bulk_at, prior, loc, val, scale, X, gram, pv, locs, hxs, hxr, gl, rs, part, zr, total,
                  local_sem, bulk_s, bulk_r, loc_s, loc_r, hx_s, hx_r, rs_s, rs_r, z_s, z_r, ag_s, ag_r):
    me = lax.axis_index("member")
    g = lax.axis_index("grid")
    row = pl.multiple_of(me * B, B)

    def bulk(r):
        p = peer_of(me, r)
        return pltpu.make_async_remote_copy(
            src_ref=prior.at[:, :, pl.ds(pl.multiple_of(p * C, C), C)], dst_ref=X.at[pl.ds(row, B)],
            send_sem=bulk_s.at[r], recv_sem=bulk_r.at[r], device_id=at_member(p), device_id_type=MESH)

    def send_bulk(stage):
        for r in ORDER[bulk_at[stage]:bulk_at[stage + 1]]:
            bulk(r).start()

    def plane(src, dst, s, t, r):
        p = peer_of(me, r)
        return pltpu.make_async_remote_copy(
            src_ref=src(p), dst_ref=dst, send_sem=s.at[r], recv_sem=t.at[r],
            device_id=at_member(p), device_id_type=MESH)

    load = pltpu.make_async_copy(prior, pv, local_sem.at[0])
    load.start()

    bar = pltpu.get_barrier_semaphore()

    @pl.loop(1, G)
    def _(r):
        pl.semaphore_signal(bar, inc=1, device_id=at_member(peer_of(me, r)), device_id_type=MESH)

    @pl.loop(1, Z)
    def _(d):
        pl.semaphore_signal(bar, inc=1, device_id=at_grid((g + d) % Z), device_id_type=MESH)

    pl.semaphore_wait(bar, G - 1 + Z - 1)

    def loc_copy(r):
        return plane(lambda p: loc, locs.at[me], loc_s, loc_r, r)

    @pl.loop(1, G)
    def _(r):
        loc_copy(r).start()

    locs[me] = loc[...]
    send_bulk(0)
    load.wait()
    own = pltpu.make_async_copy(pv.at[:, :, pl.ds(pl.multiple_of(me * C, C), C)], X.at[pl.ds(row, B)], local_sem.at[1])
    own.start()

    @pl.loop(1, G)
    def _(r):
        loc_copy(r).wait()

    def hx_copy(r):
        return plane(lambda p: hxs.at[p], hxr.at[pl.ds(row, B)], hx_s, hx_r, r)

    def observe(b):
        cell = locs[b]
        lane = cell % C
        level = cell // C
        pick = (lax.broadcasted_iota(jnp.int32, (C, OBS), 0) == lane).astype(jnp.bfloat16)
        keep = lax.broadcasted_iota(jnp.int32, (R, OBS), 0) == level
        block = pv[:, :, pl.ds(pl.multiple_of(b * C, C), C)].reshape(B * R, C)
        both = jnp.dot(block, pick, preferred_element_type=jnp.float32).reshape(B, R, OBS)
        return jnp.sum(jnp.where(keep[None], both, 0.0), axis=1).astype(jnp.bfloat16)

    @pl.loop(1, G + 1)
    def _(r):
        @pl.when(r < G)
        def _():
            p = peer_of(me, r)
            hxs[p] = observe(p)

        @pl.when(r > 1)
        def _():
            hx_copy(r - 1).start()

    hxr[pl.ds(row, B), :] = observe(me)
    send_bulk(1)

    @pl.loop(1, G)
    def _(r):
        hx_copy(r).wait()

    hx = hxr[...].astype(jnp.float32)
    mean = jnp.sum(hx, axis=0, keepdims=True) * (1.0 / N)
    white = (hx - mean) * scale[...]
    innovation = (val[...] - mean) * scale[...]
    first = lax.broadcasted_iota(jnp.int32, (128, OBS), 0) == 0
    side = jnp.where(first, innovation, 0.0)
    last = (((1,), (1,)), ((), ()))
    for i in range(4):
        rows = pl.ds(i * 128, 128)
        w_i = white[i * 128:(i + 1) * 128]
        gl[rows, :N] = lax.dot_general(w_i, white, last, precision=HIGHEST, preferred_element_type=jnp.float32)
        gl[rows, N:] = lax.dot_general(w_i, side, last, precision=HIGHEST, preferred_element_type=jnp.float32)

    def rs_copy(r):
        return plane(lambda p: gl.at[pl.ds(pl.multiple_of(p * B, B), B)], rs.at[me], rs_s, rs_r, r)

    @pl.loop(1, G)
    def _(r):
        rs_copy(r).start()

    rs[me] = gl[pl.ds(row, B), :]
    send_bulk(2)

    @pl.loop(1, G)
    def _(r):
        rs_copy(r).wait()

    part[...] = lax.fori_loop(1, G, lambda i, t: t + rs[i], rs[0])

    def z_copy(d):
        return pltpu.make_async_remote_copy(
            src_ref=part, dst_ref=zr.at[g], send_sem=z_s.at[d], recv_sem=z_r.at[d],
            device_id=at_grid((g + d) % Z), device_id_type=MESH)

    zr[g] = part[...]

    @pl.loop(1, Z)
    def _(d):
        z_copy(d).start()

    send_bulk(3)

    @pl.loop(1, Z)
    def _(d):
        z_copy(d).wait()

    total[...] = lax.fori_loop(1, Z, lambda i, t: t + zr[i], zr[0])

    def ag_copy(r):
        return plane(lambda p: total, gram.at[pl.ds(row, B)], ag_s, ag_r, r)

    gram[pl.ds(row, B), :] = total[...]

    @pl.loop(1, G)
    def _(r):
        ag_copy(r).start()

    send_bulk(4)

    @pl.loop(1, G)
    def _(r):
        ag_copy(r).wait()

    own.wait()

    @pl.loop(1, G)
    def _(r):
        bulk(r).wait()


def gather_and_sum(prior, loc, val, scale, bulk_at):
    vmem = pl.BlockSpec(memory_space=pltpu.VMEM)
    anym = pl.BlockSpec(memory_space=ANY)
    dma = pltpu.SemaphoreType.DMA
    return pl.pallas_call(
        functools.partial(gather_kernel, bulk_at),
        out_shape=(jax.ShapeDtypeStruct((N, R, C), jnp.bfloat16), jax.ShapeDtypeStruct((N, EXT), jnp.float32)),
        in_specs=[anym, vmem, vmem, vmem],
        out_specs=(anym, vmem),
        scratch_shapes=[
            pltpu.VMEM((B, R, G * C), jnp.bfloat16),
            pltpu.VMEM((G, 1, OBS), jnp.int32),
            pltpu.VMEM((G, B, OBS), jnp.bfloat16),
            pltpu.VMEM((N, OBS), jnp.bfloat16),
            pltpu.VMEM((N, EXT), jnp.float32),
            pltpu.VMEM((G, B, EXT), jnp.float32),
            pltpu.VMEM((B, EXT), jnp.float32),
            pltpu.VMEM((Z, B, EXT), jnp.float32),
            pltpu.VMEM((B, EXT), jnp.float32),
            dma((2,)), dma((G,)), dma((G,)), dma((G,)), dma((G,)), dma((G,)), dma((G,)),
            dma((G,)), dma((G,)), dma((Z,)), dma((Z,)), dma((G,)), dma((G,)),
        ],
        compiler_params=pltpu.CompilerParams(collective_id=0, has_side_effects=True, vmem_limit_bytes=48 << 20),
        name="gather_and_sum",
    )(prior, loc, val, scale)


LOOSE = 0.15
TIGHT = 1e-7


def factor_kernel(gram, out, a, m, b):
    eye = (lax.broadcasted_iota(jnp.int32, (N, N), 0) == lax.broadcasted_iota(jnp.int32, (N, N), 1)).astype(jnp.float32)
    a[...] = gram[:, :N] + (N - 1.0) * eye
    diagonal = jnp.sum(a[...] * eye, axis=1, keepdims=True)
    m[...] = eye * lax.rsqrt(diagonal)
    rhs_t = (((1,), (1,)), ((), ()))

    def update(precision):
        t = jnp.dot(m[...], a[...], precision=precision, preferred_element_type=jnp.float32)
        e = lax.dot_general(t, m[...], rhs_t, precision=precision, preferred_element_type=jnp.float32)
        rows = lax.broadcasted_iota(jnp.int32, (N, N), 0)
        cols = lax.broadcasted_iota(jnp.int32, (N, N), 1)
        same = rows == cols
        e = jnp.where(same, e - 1.0, e)
        low = jnp.where(cols < rows, e, jnp.where(same, 0.5 * e, 0.0))
        m[...] -= jnp.dot(low, m[...], precision=precision, preferred_element_type=jnp.float32)
        return 2.0 * jnp.sum(low * low)

    def steps(precision, bound, most, start):
        return lax.while_loop(
            lambda s: (s[0] < most) & (s[1] > bound),
            lambda s: (s[0] + 1, update(precision)), (0, start))[1]

    left = steps(lax.Precision.DEFAULT, LOOSE, 16, jnp.float32(1e30))
    left = steps(HIGHEST, TIGHT, 8, jnp.float32(1e30))

    @pl.when(jnp.logical_not(left <= TIGHT))
    def _():
        a[...] = gram[:, :N] + (N - 1.0) * eye
        m[...] = eye

        @pl.loop(0, N)
        def _(k):
            pivot_row = a[pl.ds(k, 1), :]
            lanes = lax.broadcasted_iota(jnp.int32, (1, N), 1)
            pivot = jnp.sum(jnp.where(lanes == k, pivot_row, 0.0), axis=1, keepdims=True)
            inv = 1.0 / jnp.sqrt(pivot)
            u = pivot_row * inv
            v = m[pl.ds(k, 1), :] * inv
            m[pl.ds(k, 1), :] = v

            @pl.loop(0, N // 64)
            def _(i):
                rows = pl.ds(pl.multiple_of(i * 64, 64), 64)
                blk = a[rows, :]
                cols = lax.broadcasted_iota(jnp.int32, (64, N), 1)
                ids = lax.broadcasted_iota(jnp.int32, (64, 1), 0) + i * 64
                col = jnp.sum(jnp.where(cols == k, blk, 0.0), axis=1, keepdims=True) * inv
                col = jnp.where(ids > k, col, 0.0)
                a[rows, :] = blk - col * u
                m[rows, :] = m[rows, :] - col * v

    drive = gram[:, N:]
    inner = jnp.dot(m[...], drive, precision=HIGHEST, preferred_element_type=jnp.float32)
    weight = lax.dot_general(inner, m[...], (((0,), (0,)), ((), ())), precision=HIGHEST,
                             preferred_element_type=jnp.float32)[0:1]
    out[...] = (weight + jnp.sqrt(jnp.float32(N - 1.0)) * m[...]).astype(jnp.bfloat16)


def transform_rows(gram):
    vmem = pl.BlockSpec(memory_space=pltpu.VMEM)
    return pl.pallas_call(
        factor_kernel,
        out_shape=jax.ShapeDtypeStruct((N, N), jnp.bfloat16),
        in_specs=[vmem], out_specs=vmem,
        scratch_shapes=[pltpu.VMEM((N, N), jnp.float32)] * 3,
        compiler_params=pltpu.CompilerParams(vmem_limit_bytes=48 << 20),
        name="transform_rows",
    )(gram)


def apply_kernel(X, tt, out, xin, xf, of, ob, load_sem, own_sem, send_s, recv_s):
    me = lax.axis_index("member")

    def load(s):
        return pltpu.make_async_copy(X.at[:, pl.ds(s * SLAB, SLAB), :], xin.at[s], load_sem.at[s])

    for s in range(SLABS):
        load(s).start()

    bar = pltpu.get_barrier_semaphore()

    @pl.loop(1, G)
    def _(r):
        pl.semaphore_signal(bar, inc=1, device_id=at_member(peer_of(me, r)), device_id_type=MESH)

    pl.semaphore_wait(bar, G - 1)

    def place(s):
        return out.at[:, pl.ds(s * SLAB, SLAB), pl.ds(pl.multiple_of(me * C, C), C)]

    def rows_for(s, p):
        return ob.at[s, pl.ds(pl.multiple_of(p * B, B), B)]

    def back(s, r):
        p = peer_of(me, r)
        return pltpu.make_async_remote_copy(
            src_ref=rows_for(s, p), dst_ref=place(s), send_sem=send_s.at[s, r], recv_sem=recv_s.at[s, r],
            device_id=at_member(p), device_id_type=MESH)

    def own(s):
        return pltpu.make_async_copy(rows_for(s, me), place(s), own_sem.at[s])

    for s in range(SLABS):
        load(s).wait()
        xf[...] = xin[s].astype(jnp.float32).reshape(N * SLAB, C)

        @pl.loop(0, SLAB // 2)
        def _(h):
            parts, means = [], []
            for q in range(2):
                x = xf[pl.ds(2 * h + q, N, stride=SLAB), :]
                mean = jnp.sum(x, axis=0, keepdims=True) * (1.0 / N)
                parts.append((x - mean).astype(jnp.bfloat16))
                means.append(mean)
            inc = jnp.dot(tt[...], jnp.concatenate(parts, axis=1), preferred_element_type=jnp.float32)
            for q in range(2):
                of[pl.ds(2 * h + q, N, stride=SLAB), :] = inc[:, q * C:(q + 1) * C] + means[q]

        ob[s] = of[...].reshape(N, SLAB, C).astype(jnp.bfloat16)
        for r in ORDER:
            back(s, r).start()
        own(s).start()

    for s in range(SLABS):
        own(s).wait()

        @pl.loop(1, G)
        def _(r):
            back(s, r).wait()


def apply_and_return(X, tt):
    vmem = pl.BlockSpec(memory_space=pltpu.VMEM)
    anym = pl.BlockSpec(memory_space=ANY)
    dma = pltpu.SemaphoreType.DMA
    return pl.pallas_call(
        apply_kernel,
        out_shape=jax.ShapeDtypeStruct((B, R, G * C), jnp.bfloat16),
        in_specs=[anym, vmem], out_specs=anym,
        scratch_shapes=[
            pltpu.VMEM((SLABS, N, SLAB, C), jnp.bfloat16),
            pltpu.VMEM((N * SLAB, C), jnp.float32),
            pltpu.VMEM((N * SLAB, C), jnp.float32),
            pltpu.VMEM((SLABS, N, SLAB, C), jnp.bfloat16),
            dma((SLABS,)), dma((SLABS,)), dma((SLABS, G)), dma((SLABS, G)),
        ],
        compiler_params=pltpu.CompilerParams(collective_id=1, has_side_effects=True, vmem_limit_bytes=48 << 20),
        name="apply_and_return",
    )(X, tt)


BULK_AT = (0, 3, 5, 8, 10, 31)


def local(prior, loc, tally, reading, sigma):
    usable = (lax.broadcasted_iota(jnp.int32, (1, OBS), 1) < tally[0, 0]).astype(jnp.float32)
    X, gram = gather_and_sum(prior, loc[0], reading[0], usable / sigma[0], BULK_AT)
    return apply_and_return(X, transform_rows(gram))


def solution(mesh):
    in_specs = (
        P("member", None, "grid"),
        P("grid", "member", None),
        P("grid", "member"),
        P("grid", "member", None),
        P("grid", "member", None),
    )
    return jax.shard_map(local, mesh=mesh, in_specs=in_specs, out_specs=P("member", None, "grid"), check_vma=False)
```

time: 773 us -> 256 us (0.33); the launches traced: 763 us -> 254 us
  waiting for transfers between devices: 248 us -> 0 us
  Pallas kernels: 0 us -> 245 us
  blocking collectives: 170 us -> 0 us
  local copies, waits for them, and re-layouts: 158 us -> 7.6 us
  other arithmetic: 136 us -> 0.66 us
  matrix products: 24 us -> 0 us
  between operations: 17.3 us -> 0.68 us
  starting transfers between devices: 8.8 us -> 0 us
    pallas_call x0 -> x3, Pallas kernels: none -> 245 us  [the longest x1 140 us: gather_and_sum(): pl.pallas_call(functools.partial(gather_kernel, bulk_at), out_shape=(jax....]
    psum x1 -> x0, waiting for transfers between devices: 174 us -> none  [reduce_gram(): lax.psum((gram_local, drive_local), ('member', 'grid'))]
    another operation x18 -> x0, other arithmetic: 127 us -> none  [the longest x15 85.1 us: transform_matrix(): factor_low = jnp.linalg.cholesky(system)]
    psum x1 -> x0, blocking collectives: 89.1 us -> none  [reduce_gram(): lax.psum((gram_local, drive_local), ('member', 'grid'))]
    unnamed x19 -> x5, local copies, waits for them, and re-layouts: 90.5 us -> 7.6 us
    all_to_all x1 -> x0, blocking collectives: 81.4 us -> none  [local(): lax.all_to_all(updated, 'member', split_axis=0, concat_axis=2, tiled=True)]
    all_to_all x1 -> x0, waiting for transfers between devices: 74.8 us -> none  [local(): lax.all_to_all(prior_ensemble, 'member', split_axis=2, concat_axis=0, til...]
    all_to_all x3 -> x0, local copies, waits for them, and re-layouts: 35.8 us -> none  [the longest x1 18.8 us: local(): lax.all_to_all(prior_ensemble, 'member', split_axis=2, concat_axis=0, til...]
  transfers between devices with their start and end apart: 2 -> 0, of which waited for: 2 -> 0; matrix products, arithmetic and copies ran while one was open for 1% -> 0% of each run, Pallas kernels for 0% -> 0%
where the time goes in v1:
time: 256 us; the launch traced here: 254 us
  Pallas kernels  245 us (96%)
  local copies, waits for them, and re-layouts  7.6 us (3%)
    pallas_call x1, Pallas kernels, gather_and_sum(): pl.pallas_call(functools.partial(gather_kernel, bulk_at), out_shape=(jax....  140 us
    pallas_call x1, Pallas kernels, apply_and_return(): pl.pallas_call(apply_kernel, out_shape=jax.ShapeDtypeStruct((B, R, G * C)...  82.9 us
    pallas_call x1, Pallas kernels, transform_rows(): pl.pallas_call(factor_kernel, out_shape=jax.ShapeDtypeStruct((N, N), jnp....  22.2 us
    unnamed x5, local copies, waits for them, and re-layouts  7.6 us

profile of v1, /device:TPU:1, one launch (start us, length us, event | category | flops | bytes accessed | tf_op | source)
XLA Modules:
  0.0 254.1 jit_solution(17010814140849282128)
XLA Ops:
  0.7 0.7 fusion.scale
  1.3 0.0 copy-start
  1.3 0.7 copy-done
  2.0 0.0 copy-start.1
  2.0 0.7 copy-done.1
  2.6 140.0 %gather_and_sum.1 = (bf16[512,48,128]{2,1,0:T(8,128)(2,1)}, f32[512,640]{1,0:T(8,128)S(1)}) custom-call(bf16[16,48,4096]{2,1,0:T(8,128)(2,1)} %prior.1, s32[1,128]{1,0:T(1,128)S(1)} %bitcast.6, f32[1,128]{1,0:T(1,128)S(1)} %bitcast.7, f32[1,128]{1,0:T(1,128)S(1)} %fusion.scale), custom_call_target="tpu_custom_call" | custom-call | tf_op jit(solution)/shard_map/gather_and_sum/pallas_call | solution.py:202
  142.6 22.2 %transform_rows.1.tt = bf16[512,512]{1,0:T(8,128)(2,1)S(1)} custom-call(f32[512,640]{1,0:T(8,128)S(1)} %get-tuple-element.8.gram), custom_call_target="tpu_custom_call" | custom-call | tf_op jit(solution)/shard_map/transform_rows/pallas_call | solution.py:290
  164.9 82.9 %apply_and_return.1 = bf16[16,48,4096]{2,1,0:T(8,128)(2,1)} custom-call(bf16[512,48,128]{2,1,0:T(8,128)(2,1)} %get-tuple-element.7.X, bf16[512,512]{1,0:T(8,128)(2,1)S(1)} %transform_rows.1.tt), custom_call_target="tpu_custom_call" | custom-call | tf_op jit(solution)/shard_map/apply_and_return/pallas_call | solution.py:365
  247.8 6.3 %copy.8 = bf16[16,48,4096]{2,1,0:T(8,128)(2,1)} copy(bf16[16,48,4096]{2,1,0:T(8,128)(2,1)} %apply_and_return.1) | data formatting | bytes 12582912
Async XLA Ops:
  1.3 0.7 copy-start
  2.0 0.7 copy-start.1

commit v2 on v1

--- a/solution.py
+++ b/solution.py
@@ -21,6 +21,8 @@
 EXT = N + 128
 SLAB = 8
 SLABS = R // SLAB
+CHIPS = G // 2
+HALF = N // 2
 
 ORDER = (8, 24, 16, 2, 6, 4, 1, 9, 25, 17, 3, 7, 5, 10, 26, 18, 11, 27, 19, 12, 28, 20, 13, 29, 21, 14, 30, 22, 15, 31, 23)
 
@@ -40,21 +42,27 @@
     return {"grid": q}
 
 
-def gather_kernel(bulk_at, prior, loc, val, scale, X, gram, pv, locs, hxs, hxr, gl, rs, part, zr, total,
-                  local_sem, bulk_s, bulk_r, loc_s, loc_r, hx_s, hx_r, rs_s, rs_r, z_s, z_r, ag_s, ag_r):
+def gather_kernel(bulk_at, prior, loc, val, scale, X, gram_out, tt, left, pv, locs, hxs, hxr, gl, half, rs, part, zr,
+                  total, gram, m, local_sem, own_sem, bulk_s, bulk_r, loc_s, loc_r, hx_s, hx_r, pair_s, pair_r,
+                  rs_s, rs_r, z_s, z_r, ag_s, ag_r):
     me = lax.axis_index("member")
     g = lax.axis_index("grid")
+    chip, core = me // 2, me % 2
     row = pl.multiple_of(me * B, B)
-
-    def bulk(r):
+    mine = pl.multiple_of(core * HALF, HALF)
+    other = pl.multiple_of((1 - core) * HALF, HALF)
+    share = pl.multiple_of(core * HALF + chip * B, B)
+
+    def bulk(s, r):
         p = peer_of(me, r)
         return pltpu.make_async_remote_copy(
-            src_ref=prior.at[:, :, pl.ds(pl.multiple_of(p * C, C), C)], dst_ref=X.at[pl.ds(row, B)],
-            send_sem=bulk_s.at[r], recv_sem=bulk_r.at[r], device_id=at_member(p), device_id_type=MESH)
+            src_ref=prior.at[:, pl.ds(pl.multiple_of(s * SLAB, SLAB), SLAB), pl.ds(pl.multiple_of(p * C, C), C)],
+            dst_ref=X.at[s, pl.ds(row, B)],
+            send_sem=bulk_s.at[s, r], recv_sem=bulk_r.at[s, r], device_id=at_member(p), device_id_type=MESH)
 
     def send_bulk(stage):
-        for r in ORDER[bulk_at[stage]:bulk_at[stage + 1]]:
-            bulk(r).start()
+        for i in range(bulk_at[stage], bulk_at[stage + 1]):
+            bulk(i // (G - 1), ORDER[i % (G - 1)]).start()
 
     def plane(src, dst, s, t, r):
         p = peer_of(me, r)
@@ -87,12 +95,20 @@
     locs[me] = loc[...]
     send_bulk(0)
     load.wait()
-    own = pltpu.make_async_copy(pv.at[:, :, pl.ds(pl.multiple_of(me * C, C), C)], X.at[pl.ds(row, B)], local_sem.at[1])
-    own.start()
+
+    def own(s):
+        return pltpu.make_async_copy(
+            pv.at[:, pl.ds(pl.multiple_of(s * SLAB, SLAB), SLAB), pl.ds(pl.multiple_of(me * C, C), C)],
+            X.at[s, pl.ds(row, B)], own_sem.at[s])
+
+    for s in range(SLABS):
+        own(s).start()
 
     @pl.loop(1, G)
     def _(r):
         loc_copy(r).wait()
+
+    send_bulk(1)
 
     def hx_copy(r):
         return plane(lambda p: hxs.at[p], hxr.at[pl.ds(row, B)], hx_s, hx_r, r)
@@ -119,7 +135,7 @@
             hx_copy(r - 1).start()
 
     hxr[pl.ds(row, B), :] = observe(me)
-    send_bulk(1)
+    send_bulk(2)
 
     @pl.loop(1, G)
     def _(r):
@@ -138,21 +154,32 @@
         gl[rows, :N] = lax.dot_general(w_i, white, last, precision=HIGHEST, preferred_element_type=jnp.float32)
         gl[rows, N:] = lax.dot_general(w_i, side, last, precision=HIGHEST, preferred_element_type=jnp.float32)
 
+    def pair_copy(i, src, dst):
+        return pltpu.make_async_remote_copy(
+            src_ref=src, dst_ref=dst, send_sem=pair_s.at[i], recv_sem=pair_r.at[i],
+            device_id=at_member(chip * 2 + 1 - core), device_id_type=MESH)
+
+    swap = pair_copy(0, gl.at[pl.ds(other, HALF)], half)
+    swap.start()
+    send_bulk(3)
+    swap.wait()
+    gl[pl.ds(mine, HALF), :] += half[...]
+
     def rs_copy(r):
-        return plane(lambda p: gl.at[pl.ds(pl.multiple_of(p * B, B), B)], rs.at[me], rs_s, rs_r, r)
-
-    @pl.loop(1, G)
+        return plane(lambda p: gl.at[pl.ds(pl.multiple_of(core * HALF + (p // 2) * B, B), B)], rs.at[chip], rs_s, rs_r, 2 * r)
+
+    @pl.loop(1, CHIPS)
     def _(r):
         rs_copy(r).start()
 
-    rs[me] = gl[pl.ds(row, B), :]
-    send_bulk(2)
-
-    @pl.loop(1, G)
+    rs[chip] = gl[pl.ds(share, B), :]
+    send_bulk(4)
+
+    @pl.loop(1, CHIPS)
     def _(r):
         rs_copy(r).wait()
 
-    part[...] = lax.fori_loop(1, G, lambda i, t: t + rs[i], rs[0])
+    part[...] = lax.fori_loop(1, CHIPS, lambda i, t: t + rs[i], rs[0])
 
     def z_copy(d):
         return pltpu.make_async_remote_copy(
@@ -165,7 +192,7 @@
     def _(d):
         z_copy(d).start()
 
-    send_bulk(3)
+    send_bulk(5)
 
     @pl.loop(1, Z)
     def _(d):
@@ -174,25 +201,41 @@
     total[...] = lax.fori_loop(1, Z, lambda i, t: t + zr[i], zr[0])
 
     def ag_copy(r):
-        return plane(lambda p: total, gram.at[pl.ds(row, B)], ag_s, ag_r, r)
-
-    gram[pl.ds(row, B), :] = total[...]
-
-    @pl.loop(1, G)
+        return plane(lambda p: total, gram.at[pl.ds(share, B)], ag_s, ag_r, 2 * r)
+
+    gram[pl.ds(share, B), :] = total[...]
+
+    @pl.loop(1, CHIPS)
     def _(r):
         ag_copy(r).start()
 
-    send_bulk(4)
-
-    @pl.loop(1, G)
+    send_bulk(6)
+
+    @pl.loop(1, CHIPS)
     def _(r):
         ag_copy(r).wait()
 
-    own.wait()
-
-    @pl.loop(1, G)
-    def _(r):
-        bulk(r).wait()
+    swap = pair_copy(1, gram.at[pl.ds(mine, HALF)], gram.at[pl.ds(mine, HALF)])
+    swap.start()
+    send_bulk(7)
+    swap.wait()
+    start_factor(gram, m)
+    for _ in range(COARSE):
+        update_factor(gram, m, lax.Precision.DEFAULT)
+    keep_gram = pltpu.make_async_copy(gram, gram_out, local_sem.at[1])
+    keep_gram.start()
+    for _ in range(FINE):
+        rest = update_factor(gram, m, HIGHEST)
+    left[...] = jnp.broadcast_to(rest, (8, 128))
+    tt[...] = finish_factor(gram, m)
+
+    keep_gram.wait()
+    for s in range(SLABS):
+        own(s).wait()
+
+        @pl.loop(1, G)
+        def _(r):
+            bulk(s, r).wait()
 
 
 def gather_and_sum(prior, loc, val, scale, bulk_at):
@@ -201,107 +244,126 @@
     dma = pltpu.SemaphoreType.DMA
     return pl.pallas_call(
         functools.partial(gather_kernel, bulk_at),
-        out_shape=(jax.ShapeDtypeStruct((N, R, C), jnp.bfloat16), jax.ShapeDtypeStruct((N, EXT), jnp.float32)),
+        out_shape=(
+            jax.ShapeDtypeStruct((SLABS, N, SLAB, C), jnp.bfloat16),
+            jax.ShapeDtypeStruct((N, EXT), jnp.float32),
+            jax.ShapeDtypeStruct((N, N), jnp.bfloat16),
+            jax.ShapeDtypeStruct((8, 128), jnp.float32),
+        ),
         in_specs=[anym, vmem, vmem, vmem],
-        out_specs=(anym, vmem),
+        out_specs=(anym, anym, vmem, vmem),
         scratch_shapes=[
             pltpu.VMEM((B, R, G * C), jnp.bfloat16),
             pltpu.VMEM((G, 1, OBS), jnp.int32),
             pltpu.VMEM((G, B, OBS), jnp.bfloat16),
             pltpu.VMEM((N, OBS), jnp.bfloat16),
             pltpu.VMEM((N, EXT), jnp.float32),
-            pltpu.VMEM((G, B, EXT), jnp.float32),
+            pltpu.VMEM((HALF, EXT), jnp.float32),
+            pltpu.VMEM((CHIPS, B, EXT), jnp.float32),
             pltpu.VMEM((B, EXT), jnp.float32),
             pltpu.VMEM((Z, B, EXT), jnp.float32),
             pltpu.VMEM((B, EXT), jnp.float32),
-            dma((2,)), dma((G,)), dma((G,)), dma((G,)), dma((G,)), dma((G,)), dma((G,)),
-            dma((G,)), dma((G,)), dma((Z,)), dma((Z,)), dma((G,)), dma((G,)),
+            pltpu.VMEM((N, EXT), jnp.float32),
+            pltpu.VMEM((N, N), jnp.float32),
+            dma((2,)), dma((SLABS,)), dma((SLABS, G)), dma((SLABS, G)), dma((G,)), dma((G,)), dma((G,)), dma((G,)),
+            dma((2,)), dma((2,)), dma((G,)), dma((G,)), dma((Z,)), dma((Z,)), dma((G,)), dma((G,)),
         ],
-        compiler_params=pltpu.CompilerParams(collective_id=0, has_side_effects=True, vmem_limit_bytes=48 << 20),
+        compiler_params=pltpu.CompilerParams(collective_id=0, has_side_effects=True, vmem_limit_bytes=56 << 20),
         name="gather_and_sum",
     )(prior, loc, val, scale)
 
 
-LOOSE = 0.15
-TIGHT = 1e-7
-
-
-def factor_kernel(gram, out, a, m, b):
-    eye = (lax.broadcasted_iota(jnp.int32, (N, N), 0) == lax.broadcasted_iota(jnp.int32, (N, N), 1)).astype(jnp.float32)
-    a[...] = gram[:, :N] + (N - 1.0) * eye
-    diagonal = jnp.sum(a[...] * eye, axis=1, keepdims=True)
-    m[...] = eye * lax.rsqrt(diagonal)
-    rhs_t = (((1,), (1,)), ((), ()))
-
-    def update(precision):
-        t = jnp.dot(m[...], a[...], precision=precision, preferred_element_type=jnp.float32)
-        e = lax.dot_general(t, m[...], rhs_t, precision=precision, preferred_element_type=jnp.float32)
-        rows = lax.broadcasted_iota(jnp.int32, (N, N), 0)
-        cols = lax.broadcasted_iota(jnp.int32, (N, N), 1)
-        same = rows == cols
-        e = jnp.where(same, e - 1.0, e)
-        low = jnp.where(cols < rows, e, jnp.where(same, 0.5 * e, 0.0))
-        m[...] -= jnp.dot(low, m[...], precision=precision, preferred_element_type=jnp.float32)
-        return 2.0 * jnp.sum(low * low)
-
-    def steps(precision, bound, most, start):
-        return lax.while_loop(
-            lambda s: (s[0] < most) & (s[1] > bound),
-            lambda s: (s[0] + 1, update(precision)), (0, start))[1]
-
-    left = steps(lax.Precision.DEFAULT, LOOSE, 16, jnp.float32(1e30))
-    left = steps(HIGHEST, TIGHT, 8, jnp.float32(1e30))
-
-    @pl.when(jnp.logical_not(left <= TIGHT))
-    def _():
-        a[...] = gram[:, :N] + (N - 1.0) * eye
-        m[...] = eye
-
-        @pl.loop(0, N)
-        def _(k):
-            pivot_row = a[pl.ds(k, 1), :]
-            lanes = lax.broadcasted_iota(jnp.int32, (1, N), 1)
-            pivot = jnp.sum(jnp.where(lanes == k, pivot_row, 0.0), axis=1, keepdims=True)
-            inv = 1.0 / jnp.sqrt(pivot)
-            u = pivot_row * inv
-            v = m[pl.ds(k, 1), :] * inv
-            m[pl.ds(k, 1), :] = v
-
-            @pl.loop(0, N // 64)
-            def _(i):
-                rows = pl.ds(pl.multiple_of(i * 64, 64), 64)
-                blk = a[rows, :]
-                cols = lax.broadcasted_iota(jnp.int32, (64, N), 1)
-                ids = lax.broadcasted_iota(jnp.int32, (64, 1), 0) + i * 64
-                col = jnp.sum(jnp.where(cols == k, blk, 0.0), axis=1, keepdims=True) * inv
-                col = jnp.where(ids > k, col, 0.0)
-                a[rows, :] = blk - col * u
-                m[rows, :] = m[rows, :] - col * v
-
-    drive = gram[:, N:]
-    inner = jnp.dot(m[...], drive, precision=HIGHEST, preferred_element_type=jnp.float32)
+def diagonal_mask():
+    return lax.broadcasted_iota(jnp.int32, (N, N), 0) == lax.broadcasted_iota(jnp.int32, (N, N), 1)
+
+
+def start_factor(gram, m):
+    same = diagonal_mask()
+    a = gram[:, :N] + jnp.where(same, N - 1.0, 0.0)
+    gram[:, :N] = a
+    m[...] = jnp.where(same, lax.rsqrt(jnp.sum(jnp.where(same, a, 0.0), axis=1, keepdims=True)), 0.0)
+
+
+def update_factor(gram, m, precision):
+    t = jnp.dot(m[...], gram[:, :N], precision=precision, preferred_element_type=jnp.float32)
+    e = lax.dot_general(t, m[...], (((1,), (1,)), ((), ())), precision=precision, preferred_element_type=jnp.float32)
+    rows = lax.broadcasted_iota(jnp.int32, (N, N), 0)
+    cols = lax.broadcasted_iota(jnp.int32, (N, N), 1)
+    low = jnp.where(cols < rows, e, jnp.where(cols == rows, 0.5 * (e - 1.0), 0.0))
+    m[...] -= jnp.dot(low, m[...], preferred_element_type=jnp.float32)
+    return 2.0 * jnp.sum(low * low)
+
+
+def finish_factor(gram, m):
+    inner = jnp.dot(m[...], gram[:, N:], precision=HIGHEST, preferred_element_type=jnp.float32)
     weight = lax.dot_general(inner, m[...], (((0,), (0,)), ((), ())), precision=HIGHEST,
                              preferred_element_type=jnp.float32)[0:1]
-    out[...] = (weight + jnp.sqrt(jnp.float32(N - 1.0)) * m[...]).astype(jnp.bfloat16)
-
-
-def transform_rows(gram):
+    return (weight + jnp.sqrt(jnp.float32(N - 1.0)) * m[...]).astype(jnp.bfloat16)
+
+
+def eliminate(a, m):
+    m[...] = jnp.where(diagonal_mask(), 1.0, 0.0)
+
+    @pl.loop(0, N)
+    def _(k):
+        pivot_row = a[pl.ds(k, 1), :N]
+        lanes = lax.broadcasted_iota(jnp.int32, (1, N), 1)
+        pivot = jnp.sum(jnp.where(lanes == k, pivot_row, 0.0), axis=1, keepdims=True)
+        inv = 1.0 / jnp.sqrt(pivot)
+        u = pivot_row * inv
+        v = m[pl.ds(k, 1), :] * inv
+        m[pl.ds(k, 1), :] = v
+
+        @pl.loop(0, N // 64)
+        def _(i):
+            rows = pl.ds(pl.multiple_of(i * 64, 64), 64)
+            blk = a[rows, :N]
+            cols = lax.broadcasted_iota(jnp.int32, (64, N), 1)
+            ids = lax.broadcasted_iota(jnp.int32, (64, 1), 0) + i * 64
+            col = jnp.sum(jnp.where(cols == k, blk, 0.0), axis=1, keepdims=True) * inv
+            col = jnp.where(ids > k, col, 0.0)
+            a[rows, :N] = blk - col * u
+            m[rows, :] = m[rows, :] - col * v
+
+
+COARSE = 5
+FINE = 2
+TIGHT = 1e-5
+
+
+def settle_kernel(left, gram, tt_in, tt, a, m, result, sem):
+    @pl.when(jnp.logical_not(jnp.max(left[...]) <= TIGHT))
+    def _():
+        fetch = pltpu.make_async_copy(gram, a, sem)
+        fetch.start()
+        fetch.wait()
+        eliminate(a, m)
+        result[...] = finish_factor(a, m)
+        store = pltpu.make_async_copy(result, tt, sem)
+        store.start()
+        store.wait()
+
+
+def settle(left, gram, tt):
     vmem = pl.BlockSpec(memory_space=pltpu.VMEM)
+    anym = pl.BlockSpec(memory_space=ANY)
     return pl.pallas_call(
-        factor_kernel,
+        settle_kernel,
         out_shape=jax.ShapeDtypeStruct((N, N), jnp.bfloat16),
-        in_specs=[vmem], out_specs=vmem,
-        scratch_shapes=[pltpu.VMEM((N, N), jnp.float32)] * 3,
-        compiler_params=pltpu.CompilerParams(vmem_limit_bytes=48 << 20),
-        name="transform_rows",
-    )(gram)
+        in_specs=[vmem, anym, anym], out_specs=anym,
+        scratch_shapes=[pltpu.VMEM((N, EXT), jnp.float32), pltpu.VMEM((N, N), jnp.float32),
+                        pltpu.VMEM((N, N), jnp.bfloat16), pltpu.SemaphoreType.DMA],
+        input_output_aliases={2: 0},
+        compiler_params=pltpu.CompilerParams(vmem_limit_bytes=24 << 20),
+        name="settle",
+    )(left, gram, tt)
 
 
 def apply_kernel(X, tt, out, xin, xf, of, ob, load_sem, own_sem, send_s, recv_s):
     me = lax.axis_index("member")
 
     def load(s):
-        return pltpu.make_async_copy(X.at[:, pl.ds(s * SLAB, SLAB), :], xin.at[s], load_sem.at[s])
+        return pltpu.make_async_copy(X.at[s], xin.at[s], load_sem.at[s])
 
     for s in range(SLABS):
         load(s).start()
@@ -378,13 +440,13 @@
     )(X, tt)
 
 
-BULK_AT = (0, 3, 5, 8, 10, 31)
+BULK_AT = (0, 8, 20, 36, 44, 50, 76, 82, 186)
 
 
 def local(prior, loc, tally, reading, sigma):
     usable = (lax.broadcasted_iota(jnp.int32, (1, OBS), 1) < tally[0, 0]).astype(jnp.float32)
-    X, gram = gather_and_sum(prior, loc[0], reading[0], usable / sigma[0], BULK_AT)
-    return apply_and_return(X, transform_rows(gram))
+    X, gram, tt, left = gather_and_sum(prior, loc[0], reading[0], usable / sigma[0], BULK_AT)
+    return apply_and_return(X, settle(left, gram, tt))
 
 
 def solution(mesh):

time: 256 us -> 210 us (0.82)
  Pallas kernels: 245 us -> 196 us
  local copies, waits for them, and re-layouts: 7.6 us -> 11.1 us
    pallas_call x1, Pallas kernels: 140 us -> 114 us  [gather_and_sum(): pl.pallas_call(functools.partial(gather_kernel, bulk_at), out_shape=(jax....]
    pallas_call x1, Pallas kernels: 22.2 us -> 0.13 us  [settle(): pl.pallas_call(settle_kernel, out_shape=jax.ShapeDtypeStruct((N, N), jnp....]
    unnamed x5 -> x11, local copies, waits for them, and re-layouts: 7.6 us -> 11.1 us
where the time goes in v2:
time: 210 us; the launch traced here: 209 us
  Pallas kernels  196 us (93%)
  local copies, waits for them, and re-layouts  11.1 us (5%)
    pallas_call x1, Pallas kernels, gather_and_sum(): pl.pallas_call(functools.partial(gather_kernel, bulk_at), out_shape=(jax....  114 us
    pallas_call x1, Pallas kernels, apply_and_return(): pl.pallas_call(apply_kernel, out_shape=jax.ShapeDtypeStruct((B, R, G * C)...  81.9 us
    unnamed x11, local copies, waits for them, and re-layouts  11.1 us

profile of v2, /device:TPU:1, one launch (start us, length us, event | category | flops | bytes accessed | tf_op | source)
XLA Modules:
  0.0 209.3 jit_solution(858557150785256002)
XLA Ops:
  0.7 1.1 fusion.scale
  1.8 114.4 %gather_and_sum.1 = (bf16[6,512,8,128]{3,2,1,0:T(8,128)(2,1)}, f32[512,640]{1,0:T(8,128)}, bf16[512,512]{1,0:T(8,128)(2,1)}, f32[8,128]{1,0:T(8,128)}) custom-call(bf16[16,48,4096]{2,1,0:T(8,128)(2,1)} %prior.1, s32[1,128]{1,0:T(1,128)} %bitcast.6, f32[1,128]{1,0:T(1,128)} %bitcast.7, f32[1,128]{1,0:T(1,128)} %fusion.scale), custom_call_target="tpu_custom_call" | custom-call | tf_op jit(solution)/shard_map/gather_and_sum/pallas_call | solution.py:245
  116.2 0.0 copy-start
  116.2 1.0 copy-done
  117.2 0.0 copy-start.3
  117.2 1.3 copy-done.3
  118.5 0.0 copy-start.4
  118.5 0.7 copy-done.4
  119.2 0.1 settle.1.tt
  119.4 0.0 copy-start.1
  119.4 0.8 copy-done.1
  120.1 0.0 copy-start.2
  120.2 1.0 copy-done.2
  121.2 81.9 %apply_and_return.1 = bf16[16,48,4096]{2,1,0:T(8,128)(2,1)} custom-call(bf16[6,512,8,128]{3,2,1,0:T(8,128)(2,1)} %get-tuple-element.9.X, bf16[512,512]{1,0:T(8,128)(2,1)S(1)} %copy-done.2), custom_call_target="tpu_custom_call" | custom-call | tf_op jit(solution)/shard_map/apply_and_return/pallas_call | solution.py:427
  203.1 6.3 %copy.10 = bf16[16,48,4096]{2,1,0:T(8,128)(2,1)} copy(bf16[16,48,4096]{2,1,0:T(8,128)(2,1)} %apply_and_return.1) | data formatting | bytes 12582912
Async XLA Ops:
  116.2 1.0 copy-start
  117.2 1.3 copy-start.3
  118.5 0.7 copy-start.4
  119.4 0.8 copy-start.1
  120.1 1.0 copy-start.2

commit v3 on v2

--- a/solution.py
+++ b/solution.py
@@ -331,8 +331,12 @@
 TIGHT = 1e-5
 
 
-def settle_kernel(left, gram, tt_in, tt, a, m, result, sem):
-    @pl.when(jnp.logical_not(jnp.max(left[...]) <= TIGHT))
+def settle_kernel(left, gram, tt_in, tt, rest, a, m, result, sem):
+    look = pltpu.make_async_copy(left, rest, sem)
+    look.start()
+    look.wait()
+
+    @pl.when(jnp.logical_not(jnp.max(rest[...]) <= TIGHT))
     def _():
         fetch = pltpu.make_async_copy(gram, a, sem)
         fetch.start()
@@ -345,27 +349,29 @@
 
 
 def settle(left, gram, tt):
-    vmem = pl.BlockSpec(memory_space=pltpu.VMEM)
-    anym = pl.BlockSpec(memory_space=ANY)
+    anym = pl.BlockSpec(memory_space=pltpu.HBM)
     return pl.pallas_call(
         settle_kernel,
         out_shape=jax.ShapeDtypeStruct((N, N), jnp.bfloat16),
-        in_specs=[vmem, anym, anym], out_specs=anym,
-        scratch_shapes=[pltpu.VMEM((N, EXT), jnp.float32), pltpu.VMEM((N, N), jnp.float32),
+        in_specs=[anym, anym, anym], out_specs=anym,
+        scratch_shapes=[pltpu.VMEM((8, 128), jnp.float32), pltpu.VMEM((N, EXT), jnp.float32), pltpu.VMEM((N, N), jnp.float32),
                         pltpu.VMEM((N, N), jnp.bfloat16), pltpu.SemaphoreType.DMA],
         input_output_aliases={2: 0},
-        compiler_params=pltpu.CompilerParams(vmem_limit_bytes=24 << 20),
+        compiler_params=pltpu.CompilerParams(vmem_limit_bytes=66_900_000),
         name="settle",
     )(left, gram, tt)
 
 
-def apply_kernel(X, tt, out, xin, xf, of, ob, load_sem, own_sem, send_s, recv_s):
+def apply_kernel(X, tt_hbm, out, tt, xin, xf, of, ob, tt_sem, load_sem, own_sem, send_s, recv_s):
     me = lax.axis_index("member")
 
     def load(s):
         return pltpu.make_async_copy(X.at[s], xin.at[s], load_sem.at[s])
 
-    for s in range(SLABS):
+    load(0).start()
+    fetch = pltpu.make_async_copy(tt_hbm, tt, tt_sem)
+    fetch.start()
+    for s in range(1, SLABS):
         load(s).start()
 
     bar = pltpu.get_barrier_semaphore()
@@ -391,6 +397,7 @@
     def own(s):
         return pltpu.make_async_copy(rows_for(s, me), place(s), own_sem.at[s])
 
+    fetch.wait()
     for s in range(SLABS):
         load(s).wait()
         xf[...] = xin[s].astype(jnp.float32).reshape(N * SLAB, C)
@@ -421,26 +428,26 @@
 
 
 def apply_and_return(X, tt):
-    vmem = pl.BlockSpec(memory_space=pltpu.VMEM)
-    anym = pl.BlockSpec(memory_space=ANY)
+    hbm = pl.BlockSpec(memory_space=pltpu.HBM)
     dma = pltpu.SemaphoreType.DMA
     return pl.pallas_call(
         apply_kernel,
-        out_shape=jax.ShapeDtypeStruct((B, R, G * C), jnp.bfloat16),
-        in_specs=[anym, vmem], out_specs=anym,
+        out_shape=pltpu.VMEM((B, R, G * C), jnp.bfloat16),
+        in_specs=[hbm, hbm], out_specs=pl.BlockSpec(memory_space=pltpu.VMEM),
         scratch_shapes=[
+            pltpu.VMEM((N, N), jnp.bfloat16),
             pltpu.VMEM((SLABS, N, SLAB, C), jnp.bfloat16),
             pltpu.VMEM((N * SLAB, C), jnp.float32),
             pltpu.VMEM((N * SLAB, C), jnp.float32),
             pltpu.VMEM((SLABS, N, SLAB, C), jnp.bfloat16),
-            dma((SLABS,)), dma((SLABS,)), dma((SLABS, G)), dma((SLABS, G)),
+            dma, dma((SLABS,)), dma((SLABS,)), dma((SLABS, G)), dma((SLABS, G)),
         ],
-        compiler_params=pltpu.CompilerParams(collective_id=1, has_side_effects=True, vmem_limit_bytes=48 << 20),
+        compiler_params=pltpu.CompilerParams(collective_id=1, has_side_effects=True, vmem_limit_bytes=60_600_000),
         name="apply_and_return",
     )(X, tt)
 
 
-BULK_AT = (0, 8, 20, 36, 44, 50, 76, 82, 186)
+BULK_AT = (0, 16, 40, 60, 84, 100, 130, 146, 186)
 
 
 def local(prior, loc, tally, reading, sigma):

time: 210 us -> 200 us (0.952)
  local copies, waits for them, and re-layouts: 11.1 us -> 2.71 us
    unnamed x11 -> x1, local copies, waits for them, and re-layouts: 11.1 us -> 2.71 us
    pallas_call x1, Pallas kernels: 114 us -> 109 us  [gather_and_sum(): pl.pallas_call(functools.partial(gather_kernel, bulk_at), out_shape=(jax....]
    pallas_call x1, Pallas kernels: 81.9 us -> 84.4 us  [apply_and_return(): pl.pallas_call(apply_kernel, out_shape=pltpu.VMEM((B, R, G * C), jnp.bflo...]
where the time goes in v3:
time: 200 us; the launch traced here: 198 us
  Pallas kernels  194 us (97%)
  local copies, waits for them, and re-layouts  2.71 us (1%)
    pallas_call x1, Pallas kernels, gather_and_sum(): pl.pallas_call(functools.partial(gather_kernel, bulk_at), out_shape=(jax....  109 us
    pallas_call x1, Pallas kernels, apply_and_return(): pl.pallas_call(apply_kernel, out_shape=pltpu.VMEM((B, R, G * C), jnp.bflo...  84.4 us

profile of v3, /device:TPU:1, one launch (start us, length us, event | category | flops | bytes accessed | tf_op | source)
XLA Modules:
  0.0 198.4 jit_solution(11865146521954954177)
XLA Ops:
  0.7 1.2 fusion.scale
  1.9 108.5 %gather_and_sum.1 = (bf16[6,512,8,128]{3,2,1,0:T(8,128)(2,1)}, f32[512,640]{1,0:T(8,128)}, bf16[512,512]{1,0:T(8,128)(2,1)}, f32[8,128]{1,0:T(8,128)}) custom-call(bf16[16,48,4096]{2,1,0:T(8,128)(2,1)} %prior.1, s32[1,128]{1,0:T(1,128)} %bitcast.6, f32[1,128]{1,0:T(1,128)} %bitcast.7, f32[1,128]{1,0:T(1,128)} %fusion.scale), custom_call_target="tpu_custom_call" | custom-call | tf_op jit(solution)/shard_map/gather_and_sum/pallas_call | solution.py:245
  110.4 0.8 settle.1.tt_hbm
  111.3 84.4 %apply_and_return.1 = bf16[16,48,4096]{2,1,0:T(8,128)(2,1)S(1)} custom-call(bf16[6,512,8,128]{3,2,1,0:T(8,128)(2,1)} %get-tuple-element.9.X, bf16[512,512]{1,0:T(8,128)(2,1)} %settle.1.tt_hbm), custom_call_target="tpu_custom_call" | custom-call | tf_op jit(solution)/shard_map/apply_and_return/pallas_call | solution.py:433
  195.7 2.7 %copy.9 = bf16[16,48,4096]{2,1,0:T(8,128)(2,1)} copy(bf16[16,48,4096]{2,1,0:T(8,128)(2,1)S(1)} %apply_and_return.1) | data formatting | bytes 12582912

commit v4 on v3

--- a/solution.py
+++ b/solution.py
@@ -447,7 +447,7 @@
     )(X, tt)
 
 
-BULK_AT = (0, 16, 40, 60, 84, 100, 130, 146, 186)
+BULK_AT = (0, 14, 38, 56, 74, 84, 120, 130, 186)
 
 
 def local(prior, loc, tally, reading, sigma):

time: 200 us -> 197 us (0.985)
  Pallas kernels: 194 us -> 192 us
    pallas_call x1, Pallas kernels: 84.4 us -> 81.8 us  [apply_and_return(): pl.pallas_call(apply_kernel, out_shape=pltpu.VMEM((B, R, G * C), jnp.bflo...]
where the time goes in v4:
time: 197 us; the launch traced here: 196 us
  Pallas kernels  192 us (97%)
  local copies, waits for them, and re-layouts  2.71 us (1%)
    pallas_call x1, Pallas kernels, gather_and_sum(): pl.pallas_call(functools.partial(gather_kernel, bulk_at), out_shape=(jax....  109 us
    pallas_call x1, Pallas kernels, apply_and_return(): pl.pallas_call(apply_kernel, out_shape=pltpu.VMEM((B, R, G * C), jnp.bflo...  81.8 us

profile of v4, /device:TPU:1, one launch (start us, length us, event | category | flops | bytes accessed | tf_op | source)
XLA Modules:
  0.0 196.5 jit_solution(17853363533491215379)
XLA Ops:
  0.7 1.2 fusion.scale
  1.9 109.3 %gather_and_sum.1 = (bf16[6,512,8,128]{3,2,1,0:T(8,128)(2,1)}, f32[512,640]{1,0:T(8,128)}, bf16[512,512]{1,0:T(8,128)(2,1)}, f32[8,128]{1,0:T(8,128)}) custom-call(bf16[16,48,4096]{2,1,0:T(8,128)(2,1)} %prior.1, s32[1,128]{1,0:T(1,128)} %bitcast.6, f32[1,128]{1,0:T(1,128)} %bitcast.7, f32[1,128]{1,0:T(1,128)} %fusion.scale), custom_call_target="tpu_custom_call" | custom-call | tf_op jit(solution)/shard_map/gather_and_sum/pallas_call | solution.py:245
  111.2 0.8 settle.1.tt_hbm
  112.0 81.8 %apply_and_return.1 = bf16[16,48,4096]{2,1,0:T(8,128)(2,1)S(1)} custom-call(bf16[6,512,8,128]{3,2,1,0:T(8,128)(2,1)} %get-tuple-element.9.X, bf16[512,512]{1,0:T(8,128)(2,1)} %settle.1.tt_hbm), custom_call_target="tpu_custom_call" | custom-call | tf_op jit(solution)/shard_map/apply_and_return/pallas_call | solution.py:433
  193.8 2.7 %copy.9 = bf16[16,48,4096]{2,1,0:T(8,128)(2,1)} copy(bf16[16,48,4096]{2,1,0:T(8,128)(2,1)S(1)} %apply_and_return.1) | data formatting | bytes 12582912
